TPU v7x, 32 devices: a whole 2x2x4 slice. The times are simulated.
32 devices in a mesh: dp: 4 (over y, x), expert: 8 (over z, core).
Axes of the slice: x: 2, y: 2, z: 4, core: 2. Of those that a mesh axis runs over, the one named last changes fastest.
Arguments:
- layer_input: bfloat16 [16384, 1280], P(('dp', 'expert')), may hold values from -6 to 6
- lengths: int32 [32], P(('dp', 'expert')), may hold values from 256 to 512, as said below
- expert_ids: int32 [16384, 7], P(('dp', 'expert')), may hold values from 0 to 14, all different within a row; in each aligned block of 512 rows (0 to 511, 512 to 1023, ...) at most 240 rows name the same one
- norm1: float32 [1280], replicated, may hold values from 0.5 to 1.5
- w_qkv: bfloat16 [1280, 3840], replicated, may hold values from -0.15625 to 0.15625
- w_out: bfloat16 [1280, 1280], replicated, may hold values from -1.25 to 1.25
- norm2: float32 [1280], replicated, may hold values from 0.5 to 1.5
- w_router: bfloat16 [1280, 16], replicated, may hold values from -0.078125 to 0.078125
- w_shared_in: bfloat16 [1280, 1792], replicated, may hold values from -0.15625 to 0.15625
- w_shared_down: bfloat16 [896, 1280], replicated, may hold values from -0.1875 to 0.1875
- w_expert_in: bfloat16 [16, 1280, 1792], P('expert'), may hold values from -0.15625 to 0.15625
- w_expert_down: bfloat16 [16, 896, 1280], P('expert'), may hold values from -1.5 to 1.5
- dout: bfloat16 [16384, 1280], P(('dp', 'expert')), may hold values from -6 to 6
Outputs:
- out: bfloat16 [16384, 1280], P(('dp', 'expert'))
- grad_x: float32 [16384, 1280], P(('dp', 'expert'))
- grad_norm1: float32 [1280], P(('dp', 'expert'))
- grad_qkv: float32 [1280, 3840], P(('dp', 'expert'))
- grad_out: float32 [1280, 1280], P(('dp', 'expert'))
- grad_norm2: float32 [1280], P(('dp', 'expert'))
- grad_router: float32 [1280, 16], P(('dp', 'expert'))
- grad_shared_in: float32 [1280, 1792], P(('dp', 'expert'))
- grad_shared_down: float32 [896, 1280], P(None, ('dp', 'expert'))
- grad_expert_in: float32 [16, 1280, 1792], P('expert', 'dp')
- grad_expert_down: float32 [16, 896, 1280], P('expert', 'dp')
- counts: int32 [16], replicated
Inputs may be any that keep to these rules, and one draw needn't show every extreme that they name: `expert_ids`: each row names 7 different routed experts. Among the rows of one sequence no expert is named more than 240 times, a bound that some block reaches. `lengths`: some sequence has exactly 512 live tokens and some exactly half of 512.
All inputs are finite; a program needn't handle non-finite values.
Results may differ from a plain program's by a relative error of at most 0.015.
Values may be sent and summed in bfloat16 or wider, within the bound.
No kernel may reach another device: no remote copies, remote signals or barrier semaphores. Data moves between devices by JAX's collectives and lax.ppermute only.
A program may use at most 384 MiB of HBM per device.

v0:
```python
import jax
import jax.numpy as jnp
from jax import lax
from jax.sharding import PartitionSpec as P

HEAD_DIM = 128
NORM_EPS = 1e-06
MASK_VALUE = -1e30
QUERY_BLOCK = 512


def silu_parts(gate_in):
    sigmoid_v = jax.nn.sigmoid(gate_in)
    return (gate_in * sigmoid_v, sigmoid_v * (1.0 + gate_in * (1.0 - sigmoid_v)))


def normalize(values_in, gain_vec):
    inverse = lax.rsqrt(jnp.mean(values_in * values_in, axis=-1, keepdims=True) + NORM_EPS)
    return (values_in * inverse * gain_vec, inverse)


def norm_back(incoming, values_in, inverse, gain_vec):
    scaled = values_in * inverse
    grad_gain = jnp.sum(incoming * scaled, axis=0)
    inner_grad = incoming * gain_vec
    grad_values = inverse * (
        inner_grad - scaled * jnp.mean(inner_grad * scaled, axis=-1, keepdims=True)
    )
    return (grad_values, grad_gain)


def rope_tables(seq_slots, head_width):
    half_dim = head_width // 2
    inv_freq = 1.0 / 10000.0 ** (jnp.arange(half_dim, dtype=jnp.float32) * 2.0 / head_width)
    angles = jnp.arange(seq_slots, dtype=jnp.float32)[:, None] * inv_freq[None, :]
    return (jnp.cos(angles)[:, None, :], jnp.sin(angles)[:, None, :])


def rotate(values_in, cosine, sine_t):
    half_dim = values_in.shape[-1] // 2
    first_half = values_in[..., :half_dim]
    second_half = values_in[..., half_dim:]
    return jnp.concatenate(
        [first_half * cosine - second_half * sine_t, first_half * sine_t + second_half * cosine],
        axis=-1,
    )


def score_block(query_block, keys_in, block_start, seq_length, score_scale):
    raw_scores = (
        jnp.einsum("qhd,khd->hqk", query_block, keys_in, preferred_element_type=jnp.float32)
        * score_scale
    )
    query_pos = block_start + jnp.arange(query_block.shape[0], dtype=jnp.int32)[:, None]
    key_pos = jnp.arange(keys_in.shape[0], dtype=jnp.int32)[None, :]
    allowed = (key_pos <= query_pos) & (key_pos < seq_length)
    return jnp.where(allowed[None], raw_scores, MASK_VALUE)


def attention_forward(queries, keys_in, values_in, seq_length):
    seq_slots, heads, head_width = queries.shape
    block_rows = min(QUERY_BLOCK, seq_slots)
    score_scale = head_width ** (-0.5)

    def one_block(block_index):
        block_start = block_index * block_rows
        scores = score_block(queries, keys_in, block_start, seq_length, score_scale)
        highest = jnp.max(scores, axis=-1, keepdims=True)
        weights_exp = jnp.exp(scores - highest)
        totals = jnp.sum(weights_exp, axis=-1, keepdims=True)
        probs_low = (weights_exp / totals).astype(jnp.bfloat16)
        block_out = jnp.einsum(
            "hqk,khd->qhd", probs_low, values_in, preferred_element_type=jnp.float32
        )
        return (block_out, highest + jnp.log(totals))

    block_outs, log_norm = lax.map(one_block, jnp.arange(seq_slots // block_rows))
    return (block_outs.reshape(seq_slots, heads, head_width), log_norm)


def attention_backward(queries, keys_in, values_in, grad_attended, log_norm, seq_length):
    seq_slots, heads, head_width = queries.shape
    block_rows = min(QUERY_BLOCK, seq_slots)
    score_scale = head_width ** (-0.5)

    def one_step(carried, block_in):
        grad_keys, grad_values = carried
        block_index, block_norm = block_in
        block_start = block_index * block_rows
        scores = score_block(queries, keys_in, block_start, seq_length, score_scale)
        probs = jnp.exp(scores - block_norm)
        grad_probs = jnp.einsum(
            "qhd,khd->hqk", grad_attended, values_in, preferred_element_type=jnp.float32
        )
        row_dot = jnp.sum(grad_probs * probs, axis=-1, keepdims=True)
        grad_scores = (probs * (grad_probs - row_dot)).astype(jnp.bfloat16)
        grad_query = (
            jnp.einsum("hqk,khd->qhd", grad_scores, keys_in, preferred_element_type=jnp.float32)
            * score_scale
        )
        grad_keys = (
            grad_keys
            + jnp.einsum("hqk,qhd->khd", grad_scores, queries, preferred_element_type=jnp.float32)
            * score_scale
        )
        grad_values = grad_values + jnp.einsum(
            "hqk,qhd->khd",
            probs.astype(jnp.bfloat16),
            grad_attended,
            preferred_element_type=jnp.float32,
        )
        return ((grad_keys, grad_values), grad_query)

    zeros_kv = jnp.zeros((seq_slots, heads, head_width), jnp.float32)
    (grad_keys, grad_values), grad_queries = lax.scan(
        one_step, (zeros_kv, zeros_kv), (jnp.arange(seq_slots // block_rows), log_norm)
    )
    return (grad_queries.reshape(seq_slots, heads, head_width), grad_keys, grad_values)


def reduce_experts(grad_in_part, grad_down_part):
    return (
        lax.psum_scatter(
            grad_in_part.astype(jnp.bfloat16), "dp", scatter_dimension=1, tiled=True
        ).astype(jnp.float32),
        lax.psum_scatter(
            grad_down_part.astype(jnp.bfloat16), "dp", scatter_dimension=1, tiled=True
        ).astype(jnp.float32),
    )


def per_device(
    layer_input,
    lengths,
    expert_ids,
    norm1,
    w_qkv,
    w_out,
    norm2,
    w_router,
    w_shared_in,
    w_shared_down,
    w_expert_in,
    w_expert_down,
    dout,
):
    seq_slots, width = layer_input.shape
    top_k = expert_ids.shape[1]
    experts = w_router.shape[1]
    local_experts = w_expert_in.shape[0]
    hidden_units = w_shared_down.shape[0]
    heads = width // HEAD_DIM
    capacity = (seq_slots * top_k // (experts - 1) // 8 + 1) * 8
    seq_length = lengths[0]
    live_rows = jnp.arange(seq_slots, dtype=jnp.int32) < seq_length
    live_col = live_rows.astype(jnp.float32)[:, None]
    cosine, sine_t = rope_tables(seq_slots, HEAD_DIM)
    x_full = layer_input.astype(jnp.float32)
    h1_full, inverse_one = normalize(x_full, norm1)
    h1_low = h1_full.astype(jnp.bfloat16)
    proj_qkv = jnp.dot(h1_low, w_qkv, preferred_element_type=jnp.float32).reshape(
        seq_slots, 3, heads, HEAD_DIM
    )
    queries = rotate(proj_qkv[:, 0], cosine, sine_t).astype(jnp.bfloat16)
    keys_in = rotate(proj_qkv[:, 1], cosine, sine_t).astype(jnp.bfloat16)
    values_in = proj_qkv[:, 2].astype(jnp.bfloat16)
    attended, log_norm = attention_forward(queries, keys_in, values_in, seq_length)
    attended_low = attended.reshape(seq_slots, width).astype(jnp.bfloat16)
    branch = jnp.dot(attended_low, w_out, preferred_element_type=jnp.float32)
    x_mid = x_full + live_col * branch
    h2_full, inverse_two = normalize(x_mid, norm2)
    h2_low = h2_full.astype(jnp.bfloat16)
    logits = jnp.dot(h2_low, w_router, preferred_element_type=jnp.float32)
    router_cols = jnp.arange(experts, dtype=jnp.int32) < experts - 1
    logits = jnp.where(router_cols[None, :], logits, MASK_VALUE)
    highest = jnp.max(logits, axis=-1, keepdims=True)
    weights_exp = jnp.exp(logits - highest)
    router_probs = weights_exp / jnp.sum(weights_exp, axis=-1, keepdims=True)
    choose_table = (
        expert_ids[:, :, None] == jnp.arange(experts, dtype=jnp.int32)[None, None, :]
    ).astype(jnp.float32)
    gates = jnp.sum(choose_table * router_probs[:, None, :], axis=-1)
    shared_gu = jnp.dot(h2_low, w_shared_in, preferred_element_type=jnp.float32)
    shared_act, shared_slope = silu_parts(shared_gu[:, :hidden_units])
    shared_up = shared_gu[:, hidden_units:]
    shared_hidden = (shared_act * shared_up).astype(jnp.bfloat16)
    shared_out = jnp.dot(shared_hidden, w_shared_down, preferred_element_type=jnp.float32)
    flat_ids = expert_ids.reshape(-1)
    live_flat = jnp.repeat(live_rows, top_k)
    pick_table = (
        (flat_ids[:, None] == jnp.arange(experts, dtype=jnp.int32)[None, :]) & live_flat[:, None]
    ).astype(jnp.int32)
    slot_rank = jnp.sum((jnp.cumsum(pick_table, axis=0) - pick_table) * pick_table, axis=-1)
    slot_index = jnp.where(live_flat, flat_ids * capacity + slot_rank, experts * capacity)
    slot_source = (
        jnp.full((experts * capacity,), seq_slots * top_k, jnp.int32)
        .at[slot_index]
        .set(jnp.arange(seq_slots * top_k, dtype=jnp.int32), mode="drop")
    )
    send_rows = jnp.take(h2_low, slot_source // top_k, axis=0, mode="fill", fill_value=0).reshape(
        experts, capacity, width
    )
    counts = lax.psum(jnp.sum(pick_table, axis=0), ("dp", "expert"))
    slot_rows = lax.all_to_all(send_rows, "expert", split_axis=0, concat_axis=0, tiled=True)
    slot_count = slot_rows.shape[1]
    grouped = slot_rows.reshape(-1, local_experts, slot_count, width)
    gate_up = jnp.einsum("nscd,sdf->nscf", grouped, w_expert_in, preferred_element_type=jnp.float32)
    activation, unused_slope = silu_parts(gate_up[..., :hidden_units])
    hidden_low = (activation * gate_up[..., hidden_units:]).astype(jnp.bfloat16)
    result_rows = jnp.einsum(
        "nscf,sfd->nscd", hidden_low, w_expert_down, preferred_element_type=jnp.float32
    ).astype(jnp.bfloat16)
    returned_rows = lax.all_to_all(
        result_rows.reshape(-1, slot_count, width),
        "expert",
        split_axis=0,
        concat_axis=0,
        tiled=True,
    )
    kept_gate_up = gate_up.reshape(-1, slot_count, 2 * hidden_units)
    picked = jnp.take(
        returned_rows.reshape(-1, width), slot_index, axis=0, mode="fill", fill_value=0
    ).reshape(seq_slots, top_k, width)
    picked_full = picked.astype(jnp.float32)
    routed_out = jnp.sum(gates[:, :, None] * picked_full, axis=1)
    result = (x_mid + live_col * (shared_out + routed_out)).astype(jnp.bfloat16)
    grad_top = dout.astype(jnp.float32)
    grad_branch = live_col * grad_top
    grad_branch_low = grad_branch.astype(jnp.bfloat16)
    grad_shared_down = jnp.dot(shared_hidden.T, grad_branch_low, preferred_element_type=jnp.float32)
    grad_hidden = jnp.dot(grad_branch_low, w_shared_down.T, preferred_element_type=jnp.float32)
    grad_shared_gu = jnp.concatenate(
        [grad_hidden * shared_up * shared_slope, grad_hidden * shared_act], axis=-1
    ).astype(jnp.bfloat16)
    grad_shared_in = jnp.dot(h2_low.T, grad_shared_gu, preferred_element_type=jnp.float32)
    grad_h2 = jnp.dot(grad_shared_gu, w_shared_in.T, preferred_element_type=jnp.float32)
    grad_picked = (
        (gates[:, :, None] * grad_branch[:, None, :]).astype(jnp.bfloat16).reshape(-1, width)
    )
    grad_gates = jnp.sum(picked_full * grad_branch[:, None, :], axis=-1)
    grad_send = jnp.take(grad_picked, slot_source, axis=0, mode="fill", fill_value=0).reshape(
        experts, capacity, width
    )
    grad_recv = lax.all_to_all(grad_send, "expert", split_axis=0, concat_axis=0, tiled=True)
    owners = grad_recv.shape[0] // local_experts
    grad_result = grad_recv.reshape(owners, local_experts, capacity, width)
    rows_held = slot_rows.reshape(owners, local_experts, capacity, width)
    gate_up_held = kept_gate_up.reshape(owners, local_experts, capacity, 2 * hidden_units)
    expert_act, expert_slope = silu_parts(gate_up_held[..., :hidden_units])
    expert_up = gate_up_held[..., hidden_units:]
    expert_hidden = (expert_act * expert_up).astype(jnp.bfloat16)
    grad_expert_down = jnp.einsum(
        "nscf,nscd->sfd", expert_hidden, grad_result, preferred_element_type=jnp.float32
    )
    grad_expert_hidden = jnp.einsum(
        "nscd,sfd->nscf", grad_result, w_expert_down, preferred_element_type=jnp.float32
    )
    grad_expert_gu = jnp.concatenate(
        [grad_expert_hidden * expert_up * expert_slope, grad_expert_hidden * expert_act], axis=-1
    ).astype(jnp.bfloat16)
    grad_expert_in = jnp.einsum(
        "nscd,nscf->sdf", rows_held, grad_expert_gu, preferred_element_type=jnp.float32
    )
    grad_rows = jnp.einsum(
        "nscf,sdf->nscd", grad_expert_gu, w_expert_in, preferred_element_type=jnp.float32
    ).astype(jnp.bfloat16)
    grad_back = lax.all_to_all(
        grad_rows.reshape(-1, capacity, width), "expert", split_axis=0, concat_axis=0, tiled=True
    )
    grad_slots = jnp.take(
        grad_back.reshape(-1, width), slot_index, axis=0, mode="fill", fill_value=0
    ).reshape(seq_slots, top_k, width)
    grad_h2 = grad_h2 + jnp.sum(grad_slots.astype(jnp.float32), axis=1)
    grad_probs = jnp.sum(choose_table * grad_gates[:, :, None], axis=1)
    grad_logits = (
        router_probs * (grad_probs - jnp.sum(grad_probs * router_probs, axis=-1, keepdims=True))
    ).astype(jnp.bfloat16)
    grad_router = jnp.dot(h2_low.T, grad_logits, preferred_element_type=jnp.float32)
    grad_h2 = grad_h2 + jnp.dot(grad_logits, w_router.T, preferred_element_type=jnp.float32)
    grad_mid_norm, grad_norm2 = norm_back(grad_h2, x_mid, inverse_two, norm2)
    grad_mid = grad_top + grad_mid_norm
    grad_attn_branch = (live_col * grad_mid).astype(jnp.bfloat16)
    grad_out_weight = jnp.dot(attended_low.T, grad_attn_branch, preferred_element_type=jnp.float32)
    grad_attended = (
        jnp.dot(grad_attn_branch, w_out.T, preferred_element_type=jnp.float32)
        .astype(jnp.bfloat16)
        .reshape(seq_slots, heads, HEAD_DIM)
    )
    grad_queries, grad_keys, grad_values = attention_backward(
        queries, keys_in, values_in, grad_attended, log_norm, seq_length
    )
    grad_proj = (
        jnp.stack(
            [
                rotate(grad_queries, cosine, -sine_t),
                rotate(grad_keys, cosine, -sine_t),
                grad_values,
            ],
            axis=1,
        )
        .astype(jnp.bfloat16)
        .reshape(seq_slots, 3 * width)
    )
    grad_qkv_weight = jnp.dot(h1_low.T, grad_proj, preferred_element_type=jnp.float32)
    grad_h1 = jnp.dot(grad_proj, w_qkv.T, preferred_element_type=jnp.float32)
    grad_in_norm, grad_norm1 = norm_back(grad_h1, x_full, inverse_one, norm1)
    grad_input = grad_mid + grad_in_norm
    expert_in_sum, expert_down_sum = reduce_experts(grad_expert_in, grad_expert_down)
    norm1_sum, qkv_sum, out_sum, norm2_sum, router_sum, shared_in_sum, shared_down_sum = (
        lax.psum_scatter(grad_norm1, ("dp", "expert"), scatter_dimension=0, tiled=True),
        lax.psum_scatter(grad_qkv_weight, ("dp", "expert"), scatter_dimension=0, tiled=True),
        lax.psum_scatter(grad_out_weight, ("dp", "expert"), scatter_dimension=0, tiled=True),
        lax.psum_scatter(grad_norm2, ("dp", "expert"), scatter_dimension=0, tiled=True),
        lax.psum_scatter(grad_router, ("dp", "expert"), scatter_dimension=0, tiled=True),
        lax.psum_scatter(grad_shared_in, ("dp", "expert"), scatter_dimension=0, tiled=True),
        lax.psum_scatter(grad_shared_down, ("dp", "expert"), scatter_dimension=1, tiled=True),
    )
    return (
        result,
        grad_input,
        norm1_sum,
        qkv_sum,
        out_sum,
        norm2_sum,
        router_sum,
        shared_in_sum,
        shared_down_sum,
        expert_in_sum,
        expert_down_sum,
        counts,
    )


def solution(mesh):
    return jax.shard_map(
        per_device,
        mesh=mesh,
        in_specs=(
            P(("dp", "expert"), None),
            P(("dp", "expert")),
            P(("dp", "expert"), None),
            P(),
            P(),
            P(),
            P(),
            P(),
            P(),
            P(),
            P("expert", None, None),
            P("expert", None, None),
            P(("dp", "expert"), None),
        ),
        out_specs=(
            P(("dp", "expert"), None),
            P(("dp", "expert"), None),
            P(("dp", "expert")),
            P(("dp", "expert"), None),
            P(("dp", "expert"), None),
            P(("dp", "expert")),
            P(("dp", "expert"), None),
            P(("dp", "expert"), None),
            P(None, ("dp", "expert")),
            P("expert", "dp", None),
            P("expert", "dp", None),
            P(),
        ),
        check_vma=False,
    )
```

profile of v0, /device:TPU:0, one launch (start us, length us, event | category | flops | bytes accessed | tf_op | source)
XLA Modules:
  0.0 1830.2 jit_solution(8007353251317582185)
XLA Ops:
  22.1 8.3 reduce-window.6
  36.7 14.0 scatter_custom_fusion
  52.6 2.4 fusion.72
  55.0 8.8 fusion.63
  63.8 3.3 fusion.86
  68.5 3.2 copy.141
  71.7 3.2 copy.142
  74.9 5.5 subtract_convert_fusion.3
  80.4 3.3 fusion.87
  85.4 2.4 copy-done.1
  87.8 4.6 fusion.44
  92.5 2.3 multiply_reduce_fusion.5
  97.6 21.9 %gather_fusion = bf16[3840,1280]{1,0:T(8,128)(2,1)} fusion(bf16[512,1280]{1,0:T(8,128)(2,1)} %multiply_convert_fusion.4, s32[4096]{0:T(1024)S(1)} %copy-done.57), kind=kCustom, calls=%fused_computation.2 | custom fusion | bytes 19676160 | tf_op jit(solution)/shard_map/jit(_take)/gather | solution.py:200
  119.5 7.0 broadcast_select_fusion.1
  126.5 221.4 %all_to_all.20 = bf16[16,240,1280]{2,1,0:T(8,128)(2,1)S(1)} all-to-all(bf16[16,240,1280]{2,1,0:T(8,128)(2,1)S(1)} %broadcast_select_fusion.1), channel_id=1, replica_groups=mesh['dp'=4,'expert'=8] {'expert'}, dimensions={0} | all-to-all | bytes 19660800 | tf_op jit(solution)/shard_map/all_to_all | solution.py:204
  347.9 21.4 %convolution_bitcast_fusion = f32[8,2,240,1792]{3,2,0,1:T(8,128)} fusion(bf16[8,2,240,1280]{3,2,1,0:T(8,128)(2,1)S(1)} %bitcast.127, bf16[2,1280,1792]{2,1,0:T(8,128)(2,1)S(1)} %bitcast.139), kind=kOutput, calls=%fused_computation.20 | convolution fusion | flops 17616076800 | bytes 46530560 | tf_op jit(solution)/shard_map/nscd,sdf->nscf/dot_general | solution.py:207
  369.3 10.1 multiply_convert_fusion.1
  379.4 2.8 copy-done.20
  382.2 14.8 fusion.16
  397.0 8.1 copy.105
  405.1 5.4 all-to-all-start.1
  412.7 7.5 mul.573
  420.3 19.5 %mul.574 = f32[3584,1280]{1,0:T(8,128)} reshape(f32[512,7,1280]{2,1,0:T(8,128)} %mul.573) | data formatting | bytes 36700160 | tf_op jit(solution)/shard_map/mul | solution.py:238
  443.5 181.8 %all-to-all-done.1 = bf16[16,240,1280]{2,1,0:T(8,128)(2,1)} async-done(((bf16[16,240,1280]{2,1,0:T(8,128)(2,1)}), bf16[16,240,1280]{2,1,0:T(8,128)(2,1)}, u32[]{:S(2)}, u32[]{:S(2)}) %all-to-all-start.1) | async-done | bytes 9830432 | tf_op jit(solution)/shard_map/all_to_all | solution.py:213
  625.3 24.2 %gather_fusion.2 = bf16[3584,1280]{1,0:T(8,128)(2,1)} fusion(bf16[3840,1280]{1,0:T(8,128)(2,1)} %bitcast.17, s32[4096]{0:T(1024)S(1)} %pad_clamp_fusion.1), kind=kCustom, calls=%fused_computation.clone | custom fusion | bytes 18364416 | tf_op jit(solution)/shard_map/jit(_take)/gather | solution.py:221
  649.5 10.8 multiply_reduce_fusion.1
  664.5 11.5 multiply_convert_fusion
  676.1 25.4 %gather_fusion.1 = bf16[3840,1280]{1,0:T(8,128)(2,1)} fusion(bf16[3584,1280]{1,0:T(8,128)(2,1)} %multiply_convert_fusion, s32[4096]{0:T(1024)} %pad_clamp_fusion), kind=kCustom, calls=%fused_computation.3 | custom fusion | bytes 19676160 | tf_op jit(solution)/shard_map/jit(_take)/gather | solution.py:241
  701.4 9.6 broadcast_select_fusion
  711.0 5.2 all-to-all-start.2
  719.3 214.3 %all-to-all-done.2 = bf16[16,240,1280]{2,1,0:T(8,128)(2,1)} async-done(((bf16[16,240,1280]{2,1,0:T(8,128)(2,1)}), bf16[16,240,1280]{2,1,0:T(8,128)(2,1)}, u32[]{:S(2)}, u32[]{:S(2)}) %all-to-all-start.2) | async-done | bytes 9830432 | tf_op jit(solution)/shard_map/all_to_all | solution.py:244
  933.6 15.0 bitcast_convert_fusion.1
  948.7 26.2 %fusion.1 = (bf16[8,2,240,896]{3,2,0,1:T(8,128)(2,1)}, bf16[8,2,240,896]{3,2,0,1:T(8,128)(2,1)}) fusion(f32[8,2,240,1792]{3,2,0,1:T(8,128)} %convolution_bitcast_fusion, bf16[2,896,1280]{2,1,0:T(8,128)(2,1)} %param.26, bf16[8,2,240,1280]{3,2,1,0:T(8,128)(2,1)} %bitcast.19), kind=kOutput, calls=%fused_computation.13 | convolution fusion | flops 8852766720 | bytes 55705600 | tf_op jit(solution)/shard_map/nscd,sfd->nscf/dot_general | solution.py:255
  974.9 25.2 %bitcast_convert_fusion = bf16[2,1280,1792]{2,1,0:T(8,128)(2,1)} fusion(bf16[8,2,240,1280]{3,2,1,0:T(8,128)(2,1)} %bitcast.128, bf16[8,2,240,896]{3,2,0,1:T(8,128)(2,1)} %get-tuple-element.79, bf16[8,2,240,896]{3,2,0,1:T(8,128)(2,1)} %get-tuple-element.78), kind=kOutput, calls=%fused_computation.6 | convolution fusion | flops 17648189440 | bytes 32768000 | tf_op jit(solution)/shard_map/nscd,nscf->sdf/dot_general | solution.py:261
  1000.7 5.4 fusion.89
  1006.1 3.4 multiply_convert_fusion.6
  1010.5 3.9 fusion.54
  1014.4 25.1 %fusion.17 = bf16[8,2,240,1280]{3,2,0,1:T(8,128)(2,1)} fusion(bf16[2,1280,1792]{2,1,0:T(8,128)(2,1)} %param.25, bf16[8,2,240,896]{3,2,0,1:T(8,128)(2,1)} %get-tuple-element.79, bf16[8,2,240,896]{3,2,0,1:T(8,128)(2,1)} %get-tuple-element.78), kind=kOutput, calls=%fused_computation.43 | convolution fusion | flops 17648517120 | bytes 32768000 | tf_op jit(solution)/shard_map/nscf,sdf->nscd/dot_general | solution.py:264
  1039.6 8.5 copy.108
  1048.0 5.2 all-to-all-start.3
  1053.3 8.3 fusion.52
  1061.8 260.5 %all-to-all-done.3 = bf16[16,240,1280]{2,1,0:T(8,128)(2,1)} async-done(((bf16[16,240,1280]{2,1,0:T(8,128)(2,1)}), bf16[16,240,1280]{2,1,0:T(8,128)(2,1)}, u32[]{:S(2)}, u32[]{:S(2)}) %all-to-all-start.3) | async-done | bytes 9830432 | tf_op jit(solution)/shard_map/all_to_all | solution.py:267
  1322.3 24.3 %gather_fusion.3 = bf16[3584,1280]{1,0:T(8,128)(2,1)} fusion(bf16[3840,1280]{1,0:T(8,128)(2,1)} %bitcast.25, s32[4096]{0:T(1024)S(1)} %copy-done.52), kind=kCustom, calls=%fused_computation.1.clone | custom fusion | bytes 18364416 | tf_op jit(solution)/shard_map/jit(_take)/gather | solution.py:270
  1346.6 18.9 %select_convert_fusion = (f32[3584,1280]{1,0:T(8,128)}, f32[3584,1280]{1,0:T(8,128)}) fusion(bf16[3584,1280]{1,0:T(8,128)(2,1)} %gather_fusion.3, pred[3584]{0:T(1024)(128)(4,1)S(1)} %copy-done.61, bf16[3584,1280]{1,0:T(8,128)(2,1)} %gather_fusion.2), kind=kLoop, calls=%fused_computation.36 | loop fusion | flops 18350080 | bytes 55053824 | tf_op jit(solution)/shard_map/convert_element_type | solution.py:273
  1365.4 19.3 %reshape.325 = f32[512,7,1280]{2,1,0:T(8,128)} reshape(f32[3584,1280]{1,0:T(8,128)} %get-tuple-element.98) | data formatting | bytes 36700160 | tf_op jit(solution)/shard_map/convert_element_type | solution.py:273
  1384.7 12.3 reduce_sum.165
  1397.0 6.4 convolution_add_fusion.2
  1407.0 4.7 fusion.85
  1412.5 4.7 convolution_convert_fusion.2
  1417.3 2.6 copy.110
  1419.9 11.3 multiply_reduce_fusion.2
  1431.2 6.3 multiply_convert_fusion.2
  1437.6 2.3 multiply_bitcast_fusion.1
  1449.0 6.3 copy.121
  1455.3 12.5 fusion.61
  1468.5 38.3 %psum.7 = s32[16]{0:T(128)} all-reduce(s32[16]{0:T(128)S(1)} %copy-done.74), channel_id=1, replica_groups=mesh['dp'=4,'expert'=8] {'dp','expert'}, use_global_device_ids=true, to_apply=%region_31.33 | all-reduce | flops 16 | bytes 128 | tf_op jit(solution)/shard_map/psum | solution.py:203
  1508.1 2.9 convert_element_type.161
  1511.0 12.1 fusion.41
  1523.1 42.4 %all-reduce.4 = (f32[1280]{0:T(1024)S(1)}, f32[1280]{0:T(1024)S(1)}) all-reduce(f32[1280]{0:T(1024)S(1)} %get-tuple-element.56, f32[1280]{0:T(1024)S(1)} %get-tuple-element.54), channel_id=2, replica_groups=mesh['dp'=4,'expert'=8] {'dp','expert'}, use_global_device_ids=true, to_apply=%region_20.22.clone | all-reduce | flops 2560 | bytes 20480
  1566.7 19.3 %reshape.324 = f32[512,7,1280]{2,1,0:T(8,128)} reshape(f32[3584,1280]{1,0:T(8,128)} %get-tuple-element.99) | data formatting | bytes 36700160 | tf_op jit(solution)/shard_map/convert_element_type | solution.py:224
  1586.6 28.3 %multiply_reduce_fusion = f32[512,1280]{1,0:T(8,128)S(1)} fusion(f32[512,7,1280]{2,1,0:T(8,128)} %reshape.324, f32[512,7]{1,0:T(8,128)S(1)} %copy-done.28), kind=kLoop, calls=%fused_computation.5 | loop fusion | flops 8519680 | bytes 20985856 | tf_op jit(solution)/shard_map/reduce_sum | solution.py:225
  1615.0 2.6 fusion.35
  1620.8 4.4 convert_element_type.159
  1625.2 197.3 %reduce-scatter.11.cloned.1.call-done = f32[40,3840]{1,0:T(8,128)} async-done(((f32[1280,3840]{1,0:T(8,128)}), f32[40,3840]{1,0:T(8,128)}) %reduce-scatter.11.cloned.1.call-update) | async-done | bytes 614416 | tf_op jit(solution)/shard_map/reduce_scatter | solution.py:311
  (247 shorter events, 62.7 us)
Async XLA Ops:
  8.0 84.4 %copy-start = (bf16[1280,1280]{1,0:T(8,128)(2,1)S(1)}, bf16[1280,1280]{1,0:T(8,128)(2,1)}, u32[]{:S(2)}) copy-start(bf16[1280,1280]{1,0:T(8,128)(2,1)} %param.20) | copy-start | bytes 9830404
  15.3 48.4 %copy-start.44 = (s32[3584]{0:T(1024)}, s32[3584]{0:T(1024)S(1)}, u32[]{:S(2)}) copy-start(s32[3584]{0:T(1024)S(1)} %eq.41) | copy-start | bytes 43012
  55.0 20.0 %copy-start.25 = (f32[512,64]{1,0:T(8,128)}, f32[512,64]{1,0:T(8,128)S(1)}, u32[]{:S(2)}) copy-start(f32[512,64]{1,0:T(8,128)S(1)} %get-tuple-element.102) | copy-start | bytes 393220
  63.8 4.7 copy-start.19
  74.9 5.5 copy-start.33
  83.8 4.0 copy-start.1
  83.8 4.0 copy-start.37
  87.8 4.6 copy-start.53
  87.8 4.6 copy-start.21
  87.8 4.6 copy-start.63
  92.5 3.8 copy-start.55
  97.6 21.9 %copy-start.71 = (pred[16,240]{1,0:T(8,128)(4,1)S(1)}, pred[16,240]{1,0:T(8,128)(4,1)}, u32[]{:S(2)}) copy-start(pred[16,240]{1,0:T(8,128)(4,1)} %broadcast_in_dim.145) | copy-start | bytes 11524
  119.5 228.4 %slice-start.3 = ((s8[9175040]{0:T(1024)(128)(4,1)}), s8[4194304]{0:T(1024)(128)(4,1)S(1)}, s32[]{:S(2)}) async-start(s8[9175040]{0:T(1024)(128)(4,1)} %bitcast.138), calls=%async_computation.20 | async-start | bytes 8388608
  119.5 228.4 %slice-start.4 = ((s8[9175040]{0:T(1024)(128)(4,1)}), s8[4194304]{0:T(1024)(128)(4,1)S(1)}, s32[]{:S(2)}) async-start(s8[9175040]{0:T(1024)(128)(4,1)} %bitcast.138), calls=%async_computation.21 | async-start | bytes 8388608
  126.5 221.4 %slice-start.5 = ((s8[9175040]{0:T(1024)(128)(4,1)}), s8[786432]{0:T(1024)(128)(4,1)S(1)}, s32[]{:S(2)}) async-start(s8[9175040]{0:T(1024)(128)(4,1)} %bitcast.138), calls=%async_computation.22 | async-start | bytes 1572864
  347.9 21.4 %copy-start.18 = (bf16[16,240,1280]{2,1,0:T(8,128)(2,1)}, bf16[16,240,1280]{2,1,0:T(8,128)(2,1)S(1)}, u32[]{:S(2)}) copy-start(bf16[16,240,1280]{2,1,0:T(8,128)(2,1)S(1)} %all_to_all.20) | copy-start | bytes 29491204
  405.1 5.4 copy-start.69
  405.1 220.2 %all-to-all-start.1 = ((bf16[16,240,1280]{2,1,0:T(8,128)(2,1)}), bf16[16,240,1280]{2,1,0:T(8,128)(2,1)}, u32[]{:S(2)}, u32[]{:S(2)}) async-start(bf16[16,240,1280]{2,1,0:T(8,128)(2,1)} %bitcast.119), calls=%async_computation.1 | async-start | bytes 19660800 | tf_op jit(solution)/shard_map/all_to_all | solution.py:213
  420.3 19.5 %copy-start.45 = (s32[3584]{0:T(1024)S(1)}, s32[3584]{0:T(1024)}, u32[]{:S(2)}) copy-start(s32[3584]{0:T(1024)} %copy-done.44) | copy-start | bytes 43012
  420.3 19.5 %copy-start.48 = (s32[3584]{0:T(1024)S(1)}, s32[3584]{0:T(1024)}, u32[]{:S(2)}) copy-start(s32[3584]{0:T(1024)} %copy-done.47) | copy-start | bytes 43012
  420.3 19.5 %copy-start.62 = (pred[3584]{0:T(1024)(128)(4,1)S(1)}, pred[3584]{0:T(1024)(128)(4,1)}, u32[]{:S(2)}) copy-start(pred[3584]{0:T(1024)(128)(4,1)} %and.62) | copy-start | bytes 10756
  420.3 19.5 %copy-start.50 = (s32[3840]{0:T(1024)S(1)}, s32[3840]{0:T(1024)}, u32[]{:S(2)}) copy-start(s32[3840]{0:T(1024)} %copy-done.49) | copy-start | bytes 46084
  420.3 20.2 %copy-start.40 = (bf16[1280,16]{0,1:T(8,128)(2,1)S(1)}, bf16[1280,16]{0,1:T(8,128)(2,1)}, u32[]{:S(2)}) copy-start(bf16[1280,16]{0,1:T(8,128)(2,1)} %param.22) | copy-start | bytes 122884
  439.8 209.7 %copy-start.60 = (pred[3584]{0:T(1024)(128)(4,1)}, pred[3584]{0:T(1024)(128)(4,1)S(1)}, u32[]{:S(2)}) copy-start(pred[3584]{0:T(1024)(128)(4,1)S(1)} %get-tuple-element.74) | copy-start | bytes 10756
  439.8 209.7 %copy-start.51 = (s32[4096]{0:T(1024)}, s32[4096]{0:T(1024)S(1)}, u32[]{:S(2)}) copy-start(s32[4096]{0:T(1024)S(1)} %pad_clamp_fusion.1) | copy-start | bytes 49156
  442.9 206.6 %copy-start.65 = (f32[512]{0:T(512)}, f32[512]{0:T(512)S(1)}, u32[]{:S(2)}) copy-start(f32[512]{0:T(512)S(1)} %fusion.74) | copy-start | bytes 6148
  649.5 12.5 copy-start.46
  664.3 11.8 copy-start.27
  676.1 25.4 %copy-start.70 = (pred[16,240]{1,0:T(8,128)(4,1)S(1)}, pred[16,240]{1,0:T(8,128)(4,1)}, u32[]{:S(2)}) copy-start(pred[16,240]{1,0:T(8,128)(4,1)} %broadcast_in_dim.150) | copy-start | bytes 11524
  711.0 5.3 copy-start.36
  711.0 5.3 copy-start.39
  711.0 5.3 copy-start.59
  711.0 5.3 copy-start.66
  711.0 222.6 %all-to-all-start.2 = ((bf16[16,240,1280]{2,1,0:T(8,128)(2,1)}), bf16[16,240,1280]{2,1,0:T(8,128)(2,1)}, u32[]{:S(2)}, u32[]{:S(2)}) async-start(bf16[16,240,1280]{2,1,0:T(8,128)(2,1)} %broadcast_select_fusion), calls=%async_computation.2 | async-start | bytes 19660800 | tf_op jit(solution)/shard_map/all_to_all | solution.py:244
  716.2 790.5 %all-reduce.7.cloned.1.call-start = ((), (), s32[]{:S(2)}) async-start(), calls=%async_computation.15 | async-start | bytes 163840
  719.3 788.9 %reduce-scatter.19.cloned.1.call-start = ((), (), s32[]{:S(2)}) async-start(), calls=%async_computation.14 | async-start | bytes 5734400 | tf_op jit(solution)/shard_map/reduce_scatter | solution.py:126
  948.7 672.2 %reduce-scatter.17.cloned.1.call-start = ((), (), s32[]{:S(2)}) async-start(), calls=%async_computation.13 | async-start | bytes 11468800 | tf_op jit(solution)/shard_map/reduce_scatter | solution.py:123
  1000.2 5.9 copy-start.64
  1000.2 625.0 %reduce-scatter.21.cloned.1.call-start = ((), (), s32[]{:S(2)}) async-start(), calls=%async_computation.16 | async-start | bytes 4730880
  1000.7 5.4 copy-start.8
  1000.7 5.4 copy-start.75
  1048.0 274.3 %all-to-all-start.3 = ((bf16[16,240,1280]{2,1,0:T(8,128)(2,1)}), bf16[16,240,1280]{2,1,0:T(8,128)(2,1)}, u32[]{:S(2)}, u32[]{:S(2)}) async-start(bf16[16,240,1280]{2,1,0:T(8,128)(2,1)} %bitcast.120), calls=%async_computation.3 | async-start | bytes 19660800 | tf_op jit(solution)/shard_map/all_to_all | solution.py:267
  1053.2 572.0 %reduce-scatter.15.cloned.1.call-start = ((), (), s32[]{:S(2)}) async-start(), calls=%async_computation.12 | async-start | bytes 9461760 | tf_op jit(solution)/shard_map/reduce_scatter | solution.py:315
  1061.6 260.7 %copy-start.52 = (s32[4096]{0:T(1024)S(1)}, s32[4096]{0:T(1024)}, u32[]{:S(2)}) copy-start(s32[4096]{0:T(1024)} %copy-done.51) | copy-start | bytes 49156
  1061.6 563.6 %reduce-scatter.13.cloned.1.call-start = ((), (), s32[]{:S(2)}) async-start(), calls=%async_computation.11 | async-start | bytes 6758400 | tf_op jit(solution)/shard_map/reduce_scatter | solution.py:312
  1322.3 24.3 %copy-start.61 = (pred[3584]{0:T(1024)(128)(4,1)S(1)}, pred[3584]{0:T(1024)(128)(4,1)}, u32[]{:S(2)}) copy-start(pred[3584]{0:T(1024)(128)(4,1)} %copy-done.60) | copy-start | bytes 10756
  1397.0 6.4 copy-start.3
  1397.0 6.4 copy-start.41
  1397.0 6.4 copy-start.43
  1397.0 6.4 copy-start.56
  1397.0 6.4 copy-start.68
  1411.8 410.8 %reduce-scatter.11.cloned.1.call-start = ((), (), s32[]{:S(2)}) async-start(), calls=%async_computation.10 | async-start | bytes 20275200 | tf_op jit(solution)/shard_map/reduce_scatter | solution.py:311
  1419.9 11.3 slice-start
  1419.9 11.3 slice-start.1
  1419.9 11.3 slice-start.2
  1431.2 6.4 copy-start.15
  1431.2 6.4 copy-start.17
  1449.0 6.3 copy-start.72
  1449.0 6.3 copy-start.73
  1566.7 20.0 %copy-start.28 = (f32[512,7]{1,0:T(8,128)S(1)}, f32[512,7]{1,0:T(8,128)}, u32[]{:S(2)}) copy-start(f32[512,7]{1,0:T(8,128)} %copy-done.27) | copy-start | bytes 43012
  1586.6 28.3 %copy-start.4 = (f32[512,1280]{1,0:T(8,128)S(1)}, f32[512,1280]{1,0:T(8,128)}, u32[]{:S(2)}) copy-start(f32[512,1280]{1,0:T(8,128)} %copy-done.2) | copy-start | bytes 7864324
  1586.6 28.3 %copy-start.32 = (bf16[512,896]{1,0:T(8,128)(2,1)S(1)}, bf16[512,896]{1,0:T(8,128)(2,1)}, u32[]{:S(2)}) copy-start(bf16[512,896]{1,0:T(8,128)(2,1)} %copy-done.31) | copy-start | bytes 2752516
  1586.6 28.3 %copy-start.76 = (bf16[896,1280]{1,0:T(8,128)(2,1)S(1)}, bf16[896,1280]{1,0:T(8,128)(2,1)}, u32[]{:S(2)}) copy-start(bf16[896,1280]{1,0:T(8,128)(2,1)} %param.24) | copy-start | bytes 6881284
  1615.0 3.6 copy-start.24
  (29 other events, 54.3 us)
Sparse Core Ops, SparseCore 0:
  722.7 169.1 all-reduce.6
Sparse Core Ops, SparseCore 1:
  948.7 54.8 reduce-scatter.18
  1006.7 92.7 reduce-scatter.16
  1102.1 199.6 reduce-scatter.20
  1304.7 153.0 reduce-scatter.14
  1460.6 145.8 reduce-scatter.12
  1613.5 209.0 reduce-scatter.10
where the time goes:
time: 1840 us; the launch traced here: 1830 us
  waiting for transfers between devices  854 us (46%)
  blocking collectives  302 us (16%)
  local copies, waits for them, and re-layouts  239 us (13%)
  matrix products  233 us (13%)
  other arithmetic  167 us (9%)
    all_to_all x1, waiting for transfers between devices, per_device(): lax.all_to_all(grad_rows.reshape(-1, capacity, width), 'expert', split_ax...  260 us
    all_to_all x1, blocking collectives, per_device(): lax.all_to_all(send_rows, 'expert', split_axis=0, concat_axis=0, tiled=True)  221 us
    all_to_all x1, waiting for transfers between devices, per_device(): lax.all_to_all(grad_send, 'expert', split_axis=0, concat_axis=0, tiled=True)  214 us
    reduce_scatter x1, waiting for transfers between devices, per_device(): lax.psum_scatter(grad_qkv_weight, ('dp', 'expert'), scatter_dimension=0,...  197 us
    all_to_all x1, waiting for transfers between devices, per_device(): lax.all_to_all(result_rows.reshape(-1, slot_count, width), 'expert', spli...  182 us
    unnamed x1, blocking collectives  42.4 us
    psum x1, blocking collectives, per_device(): counts = lax.psum(jnp.sum(pick_table, axis=0), ('dp', 'expert'))  38.3 us
  transfers between devices with their start and end apart: 10, of which 4 were waited for; matrix products, arithmetic and copies ran while one was open for 20% of the time, Pallas kernels for 0%

commit v1 on v0

--- a/solution.py
+++ b/solution.py
@@ -200,7 +200,7 @@
     send_rows = jnp.take(h2_low, slot_source // top_k, axis=0, mode="fill", fill_value=0).reshape(
         experts, capacity, width
     )
-    counts = lax.psum(jnp.sum(pick_table, axis=0), ("dp", "expert"))
+    counts = lax.psum(lax.psum(jnp.sum(pick_table, axis=0), "expert"), "dp")
     slot_rows = lax.all_to_all(send_rows, "expert", split_axis=0, concat_axis=0, tiled=True)
     slot_count = slot_rows.shape[1]
     grouped = slot_rows.reshape(-1, local_experts, slot_count, width)

time: 1840 us -> 1840 us (level)
  waiting for transfers between devices: 854 us -> 881 us
  blocking collectives: 302 us -> 276 us
    psum x1 -> x2, blocking collectives: 38.3 us -> 13.8 us  [per_device(): counts = lax.psum(lax.psum(jnp.sum(pick_table, axis=0), 'expert'), 'dp')]
  transfers between devices with their start and end apart: 10 -> 10, of which waited for: 4 -> 5; matrix products, arithmetic and copies ran while one was open for 20% -> 20% of each run, Pallas kernels for 0% -> 0%
where the time goes in v1:
time: 1840 us; the launch traced here: 1830 us
  waiting for transfers between devices  881 us (48%)
  blocking collectives  276 us (15%)
  local copies, waits for them, and re-layouts  239 us (13%)
  matrix products  233 us (13%)
  other arithmetic  167 us (9%)
    all_to_all x1, waiting for transfers between devices, per_device(): lax.all_to_all(grad_rows.reshape(-1, capacity, width), 'expert', split_ax...  260 us
    all_to_all x1, blocking collectives, per_device(): lax.all_to_all(send_rows, 'expert', split_axis=0, concat_axis=0, tiled=True)  221 us
    reduce_scatter x1, waiting for transfers between devices, per_device(): lax.psum_scatter(grad_qkv_weight, ('dp', 'expert'), scatter_dimension=0,...  215 us
    all_to_all x1, waiting for transfers between devices, per_device(): lax.all_to_all(grad_send, 'expert', split_axis=0, concat_axis=0, tiled=True)  214 us
    all_to_all x1, waiting for transfers between devices, per_device(): lax.all_to_all(result_rows.reshape(-1, slot_count, width), 'expert', spli...  182 us
    unnamed x1, blocking collectives  40.4 us
  transfers between devices with their start and end apart: 10, of which 5 were waited for; matrix products, arithmetic and copies ran while one was open for 20% of the time, Pallas kernels for 0%

profile of v1, /device:TPU:0, one launch (start us, length us, event | category | flops | bytes accessed | tf_op | source)
XLA Modules:
  0.0 1830.7 jit_solution(4156918328064807847)
XLA Ops:
  22.1 8.3 reduce-window.6
  36.7 14.0 scatter_custom_fusion
  52.6 2.4 fusion.72
  55.0 8.8 fusion.63
  63.8 3.3 fusion.86
  68.5 3.2 copy.141
  71.7 3.2 copy.142
  74.9 5.4 subtract_convert_fusion.3
  80.4 3.4 fusion.87
  85.3 2.4 copy-done.1
  87.8 4.6 fusion.44
  97.5 21.9 %gather_fusion = bf16[3840,1280]{1,0:T(8,128)(2,1)} fusion(bf16[512,1280]{1,0:T(8,128)(2,1)} %multiply_convert_fusion.4, s32[4096]{0:T(1024)S(1)} %copy-done.57), kind=kCustom, calls=%fused_computation.2 | custom fusion | bytes 19676160 | tf_op jit(solution)/shard_map/jit(_take)/gather | solution.py:200
  119.5 7.0 broadcast_select_fusion.1
  126.5 221.4 %all_to_all.20 = bf16[16,240,1280]{2,1,0:T(8,128)(2,1)S(1)} all-to-all(bf16[16,240,1280]{2,1,0:T(8,128)(2,1)S(1)} %broadcast_select_fusion.1), channel_id=1, replica_groups=mesh['dp'=4,'expert'=8] {'expert'}, dimensions={0} | all-to-all | bytes 19660800 | tf_op jit(solution)/shard_map/all_to_all | solution.py:204
  347.9 21.4 %convolution_bitcast_fusion = f32[8,2,240,1792]{3,2,0,1:T(8,128)} fusion(bf16[8,2,240,1280]{3,2,1,0:T(8,128)(2,1)S(1)} %bitcast.127, bf16[2,1280,1792]{2,1,0:T(8,128)(2,1)S(1)} %bitcast.139), kind=kOutput, calls=%fused_computation.20 | convolution fusion | flops 17616076800 | bytes 46530560 | tf_op jit(solution)/shard_map/nscd,sdf->nscf/dot_general | solution.py:207
  369.3 10.1 multiply_convert_fusion.1
  379.4 2.8 copy-done.20
  382.1 14.8 fusion.16
  396.9 8.1 copy.105
  405.0 5.4 all-to-all-start.1
  412.6 7.5 mul.573
  420.2 19.4 %mul.574 = f32[3584,1280]{1,0:T(8,128)} reshape(f32[512,7,1280]{2,1,0:T(8,128)} %mul.573) | data formatting | bytes 36700160 | tf_op jit(solution)/shard_map/mul | solution.py:238
  443.4 181.8 %all-to-all-done.1 = bf16[16,240,1280]{2,1,0:T(8,128)(2,1)} async-done(((bf16[16,240,1280]{2,1,0:T(8,128)(2,1)}), bf16[16,240,1280]{2,1,0:T(8,128)(2,1)}, u32[]{:S(2)}, u32[]{:S(2)}) %all-to-all-start.1) | async-done | bytes 9830432 | tf_op jit(solution)/shard_map/all_to_all | solution.py:213
  625.2 24.2 %gather_fusion.2 = bf16[3584,1280]{1,0:T(8,128)(2,1)} fusion(bf16[3840,1280]{1,0:T(8,128)(2,1)} %bitcast.17, s32[4096]{0:T(1024)S(1)} %pad_clamp_fusion.1), kind=kCustom, calls=%fused_computation.clone | custom fusion | bytes 18364416 | tf_op jit(solution)/shard_map/jit(_take)/gather | solution.py:221
  649.4 10.8 multiply_reduce_fusion.1
  664.4 11.5 multiply_convert_fusion
  676.0 25.4 %gather_fusion.1 = bf16[3840,1280]{1,0:T(8,128)(2,1)} fusion(bf16[3584,1280]{1,0:T(8,128)(2,1)} %multiply_convert_fusion, s32[4096]{0:T(1024)} %pad_clamp_fusion), kind=kCustom, calls=%fused_computation.3 | custom fusion | bytes 19676160 | tf_op jit(solution)/shard_map/jit(_take)/gather | solution.py:241
  701.3 9.5 broadcast_select_fusion
  710.9 5.2 all-to-all-start.2
  719.2 214.3 %all-to-all-done.2 = bf16[16,240,1280]{2,1,0:T(8,128)(2,1)} async-done(((bf16[16,240,1280]{2,1,0:T(8,128)(2,1)}), bf16[16,240,1280]{2,1,0:T(8,128)(2,1)}, u32[]{:S(2)}, u32[]{:S(2)}) %all-to-all-start.2) | async-done | bytes 9830432 | tf_op jit(solution)/shard_map/all_to_all | solution.py:244
  933.5 15.0 bitcast_convert_fusion.1
  948.6 26.2 %fusion.1 = (bf16[8,2,240,896]{3,2,0,1:T(8,128)(2,1)}, bf16[8,2,240,896]{3,2,0,1:T(8,128)(2,1)}) fusion(f32[8,2,240,1792]{3,2,0,1:T(8,128)} %convolution_bitcast_fusion, bf16[2,896,1280]{2,1,0:T(8,128)(2,1)} %param.26, bf16[8,2,240,1280]{3,2,1,0:T(8,128)(2,1)} %bitcast.19), kind=kOutput, calls=%fused_computation.13 | convolution fusion | flops 8852766720 | bytes 55705600 | tf_op jit(solution)/shard_map/nscd,sfd->nscf/dot_general | solution.py:255
  974.8 25.2 %bitcast_convert_fusion = bf16[2,1280,1792]{2,1,0:T(8,128)(2,1)} fusion(bf16[8,2,240,1280]{3,2,1,0:T(8,128)(2,1)} %bitcast.128, bf16[8,2,240,896]{3,2,0,1:T(8,128)(2,1)} %get-tuple-element.79, bf16[8,2,240,896]{3,2,0,1:T(8,128)(2,1)} %get-tuple-element.78), kind=kOutput, calls=%fused_computation.6 | convolution fusion | flops 17648189440 | bytes 32768000 | tf_op jit(solution)/shard_map/nscd,nscf->sdf/dot_general | solution.py:261
  1000.6 5.4 fusion.89
  1006.0 3.4 multiply_convert_fusion.6
  1010.3 3.9 fusion.54
  1014.3 25.2 %fusion.17 = bf16[8,2,240,1280]{3,2,0,1:T(8,128)(2,1)} fusion(bf16[2,1280,1792]{2,1,0:T(8,128)(2,1)} %param.25, bf16[8,2,240,896]{3,2,0,1:T(8,128)(2,1)} %get-tuple-element.79, bf16[8,2,240,896]{3,2,0,1:T(8,128)(2,1)} %get-tuple-element.78), kind=kOutput, calls=%fused_computation.43 | convolution fusion | flops 17648517120 | bytes 32768000 | tf_op jit(solution)/shard_map/nscf,sdf->nscd/dot_general | solution.py:264
  1039.5 8.4 copy.108
  1047.9 5.2 all-to-all-start.3
  1053.2 8.3 fusion.52
  1061.7 260.2 %all-to-all-done.3 = bf16[16,240,1280]{2,1,0:T(8,128)(2,1)} async-done(((bf16[16,240,1280]{2,1,0:T(8,128)(2,1)}), bf16[16,240,1280]{2,1,0:T(8,128)(2,1)}, u32[]{:S(2)}, u32[]{:S(2)}) %all-to-all-start.3) | async-done | bytes 9830432 | tf_op jit(solution)/shard_map/all_to_all | solution.py:267
  1321.9 24.2 %gather_fusion.3 = bf16[3584,1280]{1,0:T(8,128)(2,1)} fusion(bf16[3840,1280]{1,0:T(8,128)(2,1)} %bitcast.25, s32[4096]{0:T(1024)S(1)} %copy-done.52), kind=kCustom, calls=%fused_computation.1.clone | custom fusion | bytes 18364416 | tf_op jit(solution)/shard_map/jit(_take)/gather | solution.py:270
  1346.2 18.8 %select_convert_fusion = (f32[3584,1280]{1,0:T(8,128)}, f32[3584,1280]{1,0:T(8,128)}) fusion(bf16[3584,1280]{1,0:T(8,128)(2,1)} %gather_fusion.3, pred[3584]{0:T(1024)(128)(4,1)S(1)} %copy-done.61, bf16[3584,1280]{1,0:T(8,128)(2,1)} %gather_fusion.2), kind=kLoop, calls=%fused_computation.36 | loop fusion | flops 18350080 | bytes 55053824 | tf_op jit(solution)/shard_map/convert_element_type | solution.py:273
  1365.0 19.2 %reshape.325 = f32[512,7,1280]{2,1,0:T(8,128)} reshape(f32[3584,1280]{1,0:T(8,128)} %get-tuple-element.98) | data formatting | bytes 36700160 | tf_op jit(solution)/shard_map/convert_element_type | solution.py:273
  1384.3 12.3 reduce_sum.165
  1396.6 6.4 convolution_add_fusion.2
  1406.7 4.7 fusion.85
  1412.2 4.7 convolution_convert_fusion.2
  1416.9 2.6 copy.110
  1419.5 11.3 multiply_reduce_fusion.2
  1430.8 6.3 multiply_convert_fusion.2
  1448.7 6.3 copy.121
  1455.0 12.5 fusion.61
  1468.1 5.7 psum.14
  1473.9 8.1 psum.15
  1483.4 2.9 convert_element_type.161
  1486.3 12.1 fusion.41
  1498.3 40.4 %all-reduce.4 = (f32[1280]{0:T(1024)S(1)}, f32[1280]{0:T(1024)S(1)}) all-reduce(f32[1280]{0:T(1024)S(1)} %get-tuple-element.56, f32[1280]{0:T(1024)S(1)} %get-tuple-element.54), channel_id=2, replica_groups=mesh['dp'=4,'expert'=8] {'dp','expert'}, use_global_device_ids=true, to_apply=%region_20.22.clone | all-reduce | flops 2560 | bytes 20480
  1539.9 19.3 %reshape.324 = f32[512,7,1280]{2,1,0:T(8,128)} reshape(f32[3584,1280]{1,0:T(8,128)} %get-tuple-element.99) | data formatting | bytes 36700160 | tf_op jit(solution)/shard_map/convert_element_type | solution.py:224
  1559.9 28.3 %multiply_reduce_fusion = f32[512,1280]{1,0:T(8,128)S(1)} fusion(f32[512,7,1280]{2,1,0:T(8,128)} %reshape.324, f32[512,7]{1,0:T(8,128)S(1)} %copy-done.28), kind=kLoop, calls=%fused_computation.5 | loop fusion | flops 8519680 | bytes 20985856 | tf_op jit(solution)/shard_map/reduce_sum | solution.py:225
  1588.2 2.6 fusion.35
  1593.9 4.1 convert_element_type.159
  1598.0 9.7 reduce-scatter.13.cloned.1.call-done
  1607.7 215.3 %reduce-scatter.11.cloned.1.call-done = f32[40,3840]{1,0:T(8,128)} async-done(((f32[1280,3840]{1,0:T(8,128)}), f32[40,3840]{1,0:T(8,128)}) %reduce-scatter.11.cloned.1.call-update) | async-done | bytes 614416 | tf_op jit(solution)/shard_map/reduce_scatter | solution.py:311
  (248 shorter events, 67.1 us)
Async XLA Ops:
  8.0 84.3 %copy-start = (bf16[1280,1280]{1,0:T(8,128)(2,1)S(1)}, bf16[1280,1280]{1,0:T(8,128)(2,1)}, u32[]{:S(2)}) copy-start(bf16[1280,1280]{1,0:T(8,128)(2,1)} %param.20) | copy-start | bytes 9830404
  15.4 48.4 %copy-start.44 = (s32[3584]{0:T(1024)}, s32[3584]{0:T(1024)S(1)}, u32[]{:S(2)}) copy-start(s32[3584]{0:T(1024)S(1)} %eq.41) | copy-start | bytes 43012
  55.0 19.9 %copy-start.25 = (f32[512,64]{1,0:T(8,128)}, f32[512,64]{1,0:T(8,128)S(1)}, u32[]{:S(2)}) copy-start(f32[512,64]{1,0:T(8,128)S(1)} %get-tuple-element.102) | copy-start | bytes 393220
  63.8 4.7 copy-start.19
  74.9 5.4 copy-start.33
  83.8 4.0 copy-start.1
  83.8 4.0 copy-start.37
  87.7 4.6 copy-start.53
  87.7 4.6 copy-start.21
  87.7 4.6 copy-start.63
  92.4 3.8 copy-start.55
  97.5 21.9 %copy-start.71 = (pred[16,240]{1,0:T(8,128)(4,1)S(1)}, pred[16,240]{1,0:T(8,128)(4,1)}, u32[]{:S(2)}) copy-start(pred[16,240]{1,0:T(8,128)(4,1)} %broadcast_in_dim.145) | copy-start | bytes 11524
  119.5 228.4 %slice-start.3 = ((s8[9175040]{0:T(1024)(128)(4,1)}), s8[4194304]{0:T(1024)(128)(4,1)S(1)}, s32[]{:S(2)}) async-start(s8[9175040]{0:T(1024)(128)(4,1)} %bitcast.138), calls=%async_computation.20 | async-start | bytes 8388608
  119.5 228.4 %slice-start.4 = ((s8[9175040]{0:T(1024)(128)(4,1)}), s8[4194304]{0:T(1024)(128)(4,1)S(1)}, s32[]{:S(2)}) async-start(s8[9175040]{0:T(1024)(128)(4,1)} %bitcast.138), calls=%async_computation.21 | async-start | bytes 8388608
  126.5 221.4 %slice-start.5 = ((s8[9175040]{0:T(1024)(128)(4,1)}), s8[786432]{0:T(1024)(128)(4,1)S(1)}, s32[]{:S(2)}) async-start(s8[9175040]{0:T(1024)(128)(4,1)} %bitcast.138), calls=%async_computation.22 | async-start | bytes 1572864
  347.8 21.4 %copy-start.18 = (bf16[16,240,1280]{2,1,0:T(8,128)(2,1)}, bf16[16,240,1280]{2,1,0:T(8,128)(2,1)S(1)}, u32[]{:S(2)}) copy-start(bf16[16,240,1280]{2,1,0:T(8,128)(2,1)S(1)} %all_to_all.20) | copy-start | bytes 29491204
  405.0 5.4 copy-start.69
  405.0 220.2 %all-to-all-start.1 = ((bf16[16,240,1280]{2,1,0:T(8,128)(2,1)}), bf16[16,240,1280]{2,1,0:T(8,128)(2,1)}, u32[]{:S(2)}, u32[]{:S(2)}) async-start(bf16[16,240,1280]{2,1,0:T(8,128)(2,1)} %bitcast.119), calls=%async_computation.1 | async-start | bytes 19660800 | tf_op jit(solution)/shard_map/all_to_all | solution.py:213
  420.2 19.5 %copy-start.45 = (s32[3584]{0:T(1024)S(1)}, s32[3584]{0:T(1024)}, u32[]{:S(2)}) copy-start(s32[3584]{0:T(1024)} %copy-done.44) | copy-start | bytes 43012
  420.2 19.5 %copy-start.48 = (s32[3584]{0:T(1024)S(1)}, s32[3584]{0:T(1024)}, u32[]{:S(2)}) copy-start(s32[3584]{0:T(1024)} %copy-done.47) | copy-start | bytes 43012
  420.2 19.5 %copy-start.62 = (pred[3584]{0:T(1024)(128)(4,1)S(1)}, pred[3584]{0:T(1024)(128)(4,1)}, u32[]{:S(2)}) copy-start(pred[3584]{0:T(1024)(128)(4,1)} %and.62) | copy-start | bytes 10756
  420.2 19.5 %copy-start.50 = (s32[3840]{0:T(1024)S(1)}, s32[3840]{0:T(1024)}, u32[]{:S(2)}) copy-start(s32[3840]{0:T(1024)} %copy-done.49) | copy-start | bytes 46084
  420.2 20.2 %copy-start.40 = (bf16[1280,16]{0,1:T(8,128)(2,1)S(1)}, bf16[1280,16]{0,1:T(8,128)(2,1)}, u32[]{:S(2)}) copy-start(bf16[1280,16]{0,1:T(8,128)(2,1)} %param.22) | copy-start | bytes 122884
  439.7 209.7 %copy-start.60 = (pred[3584]{0:T(1024)(128)(4,1)}, pred[3584]{0:T(1024)(128)(4,1)S(1)}, u32[]{:S(2)}) copy-start(pred[3584]{0:T(1024)(128)(4,1)S(1)} %get-tuple-element.74) | copy-start | bytes 10756
  439.7 209.7 %copy-start.51 = (s32[4096]{0:T(1024)}, s32[4096]{0:T(1024)S(1)}, u32[]{:S(2)}) copy-start(s32[4096]{0:T(1024)S(1)} %pad_clamp_fusion.1) | copy-start | bytes 49156
  442.8 206.6 %copy-start.65 = (f32[512]{0:T(512)}, f32[512]{0:T(512)S(1)}, u32[]{:S(2)}) copy-start(f32[512]{0:T(512)S(1)} %fusion.74) | copy-start | bytes 6148
  649.4 12.5 copy-start.46
  664.2 11.7 copy-start.27
  676.0 25.4 %copy-start.70 = (pred[16,240]{1,0:T(8,128)(4,1)S(1)}, pred[16,240]{1,0:T(8,128)(4,1)}, u32[]{:S(2)}) copy-start(pred[16,240]{1,0:T(8,128)(4,1)} %broadcast_in_dim.150) | copy-start | bytes 11524
  710.9 5.3 copy-start.36
  710.9 5.3 copy-start.39
  710.9 5.3 copy-start.59
  710.9 5.3 copy-start.66
  710.9 222.6 %all-to-all-start.2 = ((bf16[16,240,1280]{2,1,0:T(8,128)(2,1)}), bf16[16,240,1280]{2,1,0:T(8,128)(2,1)}, u32[]{:S(2)}, u32[]{:S(2)}) async-start(bf16[16,240,1280]{2,1,0:T(8,128)(2,1)} %broadcast_select_fusion), calls=%async_computation.2 | async-start | bytes 19660800 | tf_op jit(solution)/shard_map/all_to_all | solution.py:244
  716.1 765.9 %all-reduce.7.cloned.1.call-start = ((), (), s32[]{:S(2)}) async-start(), calls=%async_computation.15 | async-start | bytes 163840
  719.2 764.2 %reduce-scatter.19.cloned.1.call-start = ((), (), s32[]{:S(2)}) async-start(), calls=%async_computation.14 | async-start | bytes 5734400 | tf_op jit(solution)/shard_map/reduce_scatter | solution.py:126
  948.5 645.4 %reduce-scatter.17.cloned.1.call-start = ((), (), s32[]{:S(2)}) async-start(), calls=%async_computation.13 | async-start | bytes 11468800 | tf_op jit(solution)/shard_map/reduce_scatter | solution.py:123
  1000.0 5.9 copy-start.64
  1000.0 598.0 %reduce-scatter.21.cloned.1.call-start = ((), (), s32[]{:S(2)}) async-start(), calls=%async_computation.16 | async-start | bytes 4730880
  1000.6 5.4 copy-start.8
  1000.6 5.4 copy-start.75
  1047.9 274.0 %all-to-all-start.3 = ((bf16[16,240,1280]{2,1,0:T(8,128)(2,1)}), bf16[16,240,1280]{2,1,0:T(8,128)(2,1)}, u32[]{:S(2)}, u32[]{:S(2)}) async-start(bf16[16,240,1280]{2,1,0:T(8,128)(2,1)} %bitcast.120), calls=%async_computation.3 | async-start | bytes 19660800 | tf_op jit(solution)/shard_map/all_to_all | solution.py:267
  1053.1 544.9 %reduce-scatter.15.cloned.1.call-start = ((), (), s32[]{:S(2)}) async-start(), calls=%async_computation.12 | async-start | bytes 9461760 | tf_op jit(solution)/shard_map/reduce_scatter | solution.py:315
  1061.5 260.5 %copy-start.52 = (s32[4096]{0:T(1024)S(1)}, s32[4096]{0:T(1024)}, u32[]{:S(2)}) copy-start(s32[4096]{0:T(1024)} %copy-done.51) | copy-start | bytes 49156
  1061.5 546.2 %reduce-scatter.13.cloned.1.call-start = ((), (), s32[]{:S(2)}) async-start(), calls=%async_computation.11 | async-start | bytes 6758400 | tf_op jit(solution)/shard_map/reduce_scatter | solution.py:312
  1321.9 24.2 %copy-start.61 = (pred[3584]{0:T(1024)(128)(4,1)S(1)}, pred[3584]{0:T(1024)(128)(4,1)}, u32[]{:S(2)}) copy-start(pred[3584]{0:T(1024)(128)(4,1)} %copy-done.60) | copy-start | bytes 10756
  1396.5 6.4 copy-start.3
  1396.5 6.4 copy-start.41
  1396.5 6.4 copy-start.43
  1396.5 6.4 copy-start.56
  1396.5 6.4 copy-start.68
  1411.4 411.6 %reduce-scatter.11.cloned.1.call-start = ((), (), s32[]{:S(2)}) async-start(), calls=%async_computation.10 | async-start | bytes 20275200 | tf_op jit(solution)/shard_map/reduce_scatter | solution.py:311
  1419.5 11.3 slice-start
  1419.5 11.3 slice-start.1
  1419.5 11.3 slice-start.2
  1430.8 6.4 copy-start.15
  1430.8 6.4 copy-start.17
  1448.7 6.3 copy-start.72
  1448.7 6.3 copy-start.73
  1539.9 19.9 %copy-start.28 = (f32[512,7]{1,0:T(8,128)S(1)}, f32[512,7]{1,0:T(8,128)}, u32[]{:S(2)}) copy-start(f32[512,7]{1,0:T(8,128)} %copy-done.27) | copy-start | bytes 43012
  1559.9 28.3 %copy-start.4 = (f32[512,1280]{1,0:T(8,128)S(1)}, f32[512,1280]{1,0:T(8,128)}, u32[]{:S(2)}) copy-start(f32[512,1280]{1,0:T(8,128)} %copy-done.2) | copy-start | bytes 7864324
  1559.9 28.3 %copy-start.32 = (bf16[512,896]{1,0:T(8,128)(2,1)S(1)}, bf16[512,896]{1,0:T(8,128)(2,1)}, u32[]{:S(2)}) copy-start(bf16[512,896]{1,0:T(8,128)(2,1)} %copy-done.31) | copy-start | bytes 2752516
  1559.9 28.3 %copy-start.76 = (bf16[896,1280]{1,0:T(8,128)(2,1)S(1)}, bf16[896,1280]{1,0:T(8,128)(2,1)}, u32[]{:S(2)}) copy-start(bf16[896,1280]{1,0:T(8,128)(2,1)} %param.24) | copy-start | bytes 6881284
  1588.2 3.4 copy-start.24
  (29 other events, 54.3 us)
Sparse Core Ops, SparseCore 0:
  722.5 169.2 all-reduce.6
Sparse Core Ops, SparseCore 1:
  948.6 54.8 reduce-scatter.18
  1006.5 92.7 reduce-scatter.16
  1102.0 199.7 reduce-scatter.20
  1304.6 153.8 reduce-scatter.14
  1461.4 146.2 reduce-scatter.12
  1614.7 208.2 reduce-scatter.10
